TPU v7x, 256 devices: a whole 4x4x8 slice. The times are simulated.
256 devices in a mesh: wide: 16 (over y_lo, z), row: 16 (over y_hi, x, core).
Axes of the slice: x: 4, y: 4 (y_hi: 2, y_lo: 2; y = y_hi * 2 + y_lo), z: 8, core: 2. Of those that a mesh axis runs over, the one named last changes fastest.
Arguments:
- hessian: float32 [18432, 18432], P('row', 'wide'), as said below
- weight: bfloat16 [4608, 18432], P('row', 'wide'), may hold values from -6 to 6
- pairs: int32 [2], replicated, may hold values from 0 to 47, as said below
Outputs:
- pruned_hessian: float32 [18432, 18432], P('row', 'wide')
- pruned_weight: bfloat16 [4608, 18432], P('row', 'wide')
Inputs may be any that keep to these rules, and one draw needn't show every extreme that they name: Two different head pairs, one of which is the last pair, 47. `hessian`: symmetric positive definite.
All inputs are finite; a program needn't handle non-finite values.
Results may differ from a plain program's by a relative error of at most 0.001.
Values may be sent and summed in bfloat16 or wider, within the bound.
A program may use at most 128 MiB of HBM per device.

v0:
```python
import jax
import jax.numpy as jnp
from jax import lax
from jax.sharding import PartitionSpec as P

HEAD = 192


def broadcast(value, axis, source):
    kept = jnp.where(lax.axis_index(axis) == source, value, 0).astype(value.dtype)
    return lax.psum(kept, axis)


def per_device(hessian, weight, pairs):
    tile_rows, tile_cols = hessian.shape
    pair_width = 2 * HEAD
    row_here = lax.axis_index("row")
    highest = lax.Precision.HIGHEST
    pair_one = pairs[0]
    pair_two = pairs[1]

    def where_is(pair_index, extent):
        start_col = pair_index * pair_width
        return (start_col // extent, start_col % extent)

    def column_panel(matrix, pair_index):
        holder, offset = where_is(pair_index, tile_cols)
        local_cols = lax.dynamic_slice_in_dim(matrix, offset, pair_width, 1)
        return broadcast(local_cols, "wide", holder)

    def solved_rows(matrix, panel, pair_index):
        holder, offset = where_is(pair_index, tile_rows)
        pivot_block = lax.dynamic_slice_in_dim(panel, offset, pair_width, 0)
        pivot_block = jnp.where(
            row_here == holder, pivot_block, jnp.eye(pair_width, dtype=jnp.float32)
        )
        rows_local = lax.dynamic_slice_in_dim(matrix, offset, pair_width, 0)
        factor = jnp.linalg.cholesky(pivot_block)
        solved = jax.scipy.linalg.cho_solve((factor, True), rows_local)
        return broadcast(solved, "row", holder)

    panel_one = column_panel(hessian, pair_one)
    solved_one = solved_rows(hessian, panel_one, pair_one)
    holder_one, offset_one = where_is(pair_one, tile_cols)
    weight_one = broadcast(
        lax.dynamic_slice_in_dim(weight, offset_one, pair_width, 1), "wide", holder_one
    )
    updated = hessian - jnp.dot(panel_one, solved_one, precision=highest)
    carried = weight.astype(jnp.float32) - jnp.dot(
        weight_one.astype(jnp.float32), solved_one, precision=highest
    )
    panel_two = column_panel(updated, pair_two)
    solved_two = solved_rows(updated, panel_two, pair_two)
    holder_two, offset_two = where_is(pair_two, tile_cols)
    weight_two = broadcast(
        lax.dynamic_slice_in_dim(carried, offset_two, pair_width, 1), "wide", holder_two
    )
    pruned_hessian = updated - jnp.dot(panel_two, solved_two, precision=highest)
    pruned_weight = (carried - jnp.dot(weight_two, solved_two, precision=highest)).astype(
        jnp.bfloat16
    )
    return (pruned_hessian, pruned_weight)


def solution(mesh):
    return jax.shard_map(
        per_device,
        mesh=mesh,
        in_specs=(P("row", "wide"), P("row", "wide"), P()),
        out_specs=(P("row", "wide"), P("row", "wide")),
        check_vma=False,
    )
```

profile of v0, /device:TPU:7, one launch (start us, length us, event | category | flops | bytes accessed | tf_op | source)
XLA Modules:
  0.0 914.7 jit_solution(16918178659369243016)
XLA Ops:
  9.2 6.9 copy.7
  16.1 2.9 dynamic-slice_select_fusion.1
  20.9 131.7 %all-reduce.8.cloned.1.call-done = f32[1152,384]{0,1:T(8,128)} async-done(((f32[1152,384]{0,1:T(8,128)}), f32[1152,384]{0,1:T(8,128)}) %all-reduce.8.cloned.1.call-update) | async-done | bytes 1769488 | tf_op jit(solution)/shard_map/psum | solution.py:11
  154.5 11.7 %cholesky.208 = f32[128,128]{1,0:T(8,128)S(1)} custom-call(f32[128,128]{1,0:T(8,128)S(1)} %cholesky.310), custom_call_target="Cholesky" | custom-call | tf_op jit(solution)/shard_map/jit(cholesky)/cholesky | solution.py:38
  166.2 9.8 %custom-call.22 = f32[1,128,128]{1,2,0:T(8,128)S(1)} custom-call(f32[1,128,128]{2,1,0:T(8,128)S(1)} %get-tuple-element.57), custom_call_target="InvertDiagBlocksLowerTriangular" | custom-call | tf_op jit(solution)/shard_map/jit(cholesky)/cholesky | solution.py:38
  176.6 11.7 %cholesky.227 = f32[128,128]{1,0:T(8,128)S(1)} custom-call(f32[128,128]{1,0:T(8,128)S(1)} %cholesky.314), custom_call_target="Cholesky" | custom-call | tf_op jit(solution)/shard_map/jit(cholesky)/cholesky | solution.py:38
  188.4 10.0 %custom-call.23 = f32[1,128,128]{1,2,0:T(8,128)S(1)} custom-call(f32[1,128,128]{2,1,0:T(8,128)S(1)} %get-tuple-element.54), custom_call_target="InvertDiagBlocksLowerTriangular" | custom-call | tf_op jit(solution)/shard_map/jit(cholesky)/cholesky | solution.py:38
  198.8 11.7 %cholesky.246 = f32[128,128]{1,0:T(8,128)S(1)} custom-call(f32[128,128]{1,0:T(8,128)S(1)} %convolution_subtract_fusion.15), custom_call_target="Cholesky" | custom-call | tf_op jit(solution)/shard_map/jit(cholesky)/cholesky | solution.py:38
  214.0 6.1 while.4
  220.1 29.5 %custom-call.24 = f32[3,128,128]{1,2,0:T(8,128)S(1)} custom-call(f32[3,128,128]{2,1,0:T(8,128)S(1)} %get-tuple-element.18), custom_call_target="InvertDiagBlocksLowerTriangular" | custom-call | tf_op jit(solution)/shard_map/jit(_cho_solve)/triangular_solve | solution.py:39
  262.1 26.1 %all-reduce.14.cloned.1.call-done = bf16[288,384]{1,0:T(8,128)(2,1)} async-done(((bf16[288,384]{1,0:T(8,128)(2,1)}), bf16[288,384]{1,0:T(8,128)(2,1)}) %all-reduce.14.cloned.1.call-update) | async-done | bytes 221200 | tf_op jit(solution)/shard_map/psum | solution.py:11
  288.2 159.2 %all-reduce.10.cloned.1.call-done = f32[384,1152]{1,0:T(8,128)} async-done(((f32[384,1152]{1,0:T(8,128)}), f32[384,1152]{1,0:T(8,128)}) %all-reduce.10.cloned.1.call-update) | async-done | bytes 1769488 | tf_op jit(solution)/shard_map/psum | solution.py:11
  447.4 3.2 convolution_subtract_fusion.2
  451.6 12.4 %convolution_subtract_fusion.1 = f32[1152,1152]{0,1:T(8,128)S(1)} fusion(f32[1152,1152]{0,1:T(8,128)} %copy.7, f32[1152,384]{0,1:T(8,128)S(1)} %copy-done.1, f32[384,1152]{1,0:T(8,128)S(1)} %copy-done.3), kind=kOutput, calls=%fused_computation.5 | convolution fusion | flops 6116622336 | bytes 14155776 | tf_op jit(solution)/shard_map/dot_general | solution.py:48
  464.0 2.4 copy-done
  468.0 132.8 %all-reduce.16.cloned.1.call-done = (f32[1152,384]{0,1:T(8,128)}, f32[288,384]{1,0:T(8,128)}) async-done(((f32[1152,384]{0,1:T(8,128)}, f32[288,384]{1,0:T(8,128)}), (f32[1152,384]{0,1:T(8,128)}, f32[288,384]{1,0:T(8,128)})) %all-reduce.16.cloned.1.call-update) | async-done | bytes 2211856 | tf_op jit(solution)/shard_map/psum | solution.py:11
  600.8 2.2 convert_select_fusion
  607.3 11.7 %cholesky.261 = f32[128,128]{1,0:T(8,128)S(1)} custom-call(f32[128,128]{1,0:T(8,128)S(1)} %cholesky.318), custom_call_target="Cholesky" | custom-call | tf_op jit(solution)/shard_map/jit(cholesky)/cholesky | solution.py:38
  619.7 9.8 %custom-call.25 = f32[1,128,128]{1,2,0:T(8,128)S(1)} custom-call(f32[1,128,128]{2,1,0:T(8,128)S(1)} %get-tuple-element.50), custom_call_target="InvertDiagBlocksLowerTriangular" | custom-call | tf_op jit(solution)/shard_map/jit(cholesky)/cholesky | solution.py:38
  633.3 11.7 %cholesky.280 = f32[128,128]{1,0:T(8,128)S(1)} custom-call(f32[128,128]{1,0:T(8,128)S(1)} %cholesky.322), custom_call_target="Cholesky" | custom-call | tf_op jit(solution)/shard_map/jit(cholesky)/cholesky | solution.py:38
  646.4 10.0 %custom-call.26 = f32[1,128,128]{1,2,0:T(8,128)S(1)} custom-call(f32[1,128,128]{2,1,0:T(8,128)S(1)} %get-tuple-element.47), custom_call_target="InvertDiagBlocksLowerTriangular" | custom-call | tf_op jit(solution)/shard_map/jit(cholesky)/cholesky | solution.py:38
  658.5 11.7 %cholesky.299 = f32[128,128]{1,0:T(8,128)S(1)} custom-call(f32[128,128]{1,0:T(8,128)S(1)} %convolution_subtract_fusion.14), custom_call_target="Cholesky" | custom-call | tf_op jit(solution)/shard_map/jit(cholesky)/cholesky | solution.py:38
  675.4 8.5 while.5
  676.1 2.2 bitcast_dynamic-update-slice_fusion.5
  683.9 29.5 %custom-call.27 = f32[3,128,128]{1,2,0:T(8,128)S(1)} custom-call(f32[3,128,128]{2,1,0:T(8,128)S(1)} %get-tuple-element.19), custom_call_target="InvertDiagBlocksLowerTriangular" | custom-call | tf_op jit(solution)/shard_map/jit(_cho_solve)/triangular_solve | solution.py:39
  713.5 2.2 fusion.13
  715.7 2.5 convolution_subtract_fusion.7
  719.0 3.1 convolution_subtract_fusion.6
  727.6 157.2 %all-reduce.12.cloned.1.call-done = f32[384,1152]{1,0:T(8,128)} async-done(((f32[384,1152]{1,0:T(8,128)}), f32[384,1152]{1,0:T(8,128)}) %all-reduce.12.cloned.1.call-update) | async-done | bytes 1769488 | tf_op jit(solution)/shard_map/psum | solution.py:11
  884.7 12.7 %convolution_subtract_fusion = f32[1152,1152]{0,1:T(8,128)} fusion(f32[1152,1152]{0,1:T(8,128)} %copy-done, f32[1152,384]{0,1:T(8,128)S(1)} %copy-done.2, f32[384,1152]{1,0:T(8,128)} %all-reduce.12.cloned.1.call-done), kind=kOutput, calls=%fused_computation.4 | convolution fusion | flops 6116622336 | bytes 14155776 | tf_op jit(solution)/shard_map/dot_general | solution.py:58
  897.4 7.0 copy.11
  904.5 3.3 fusion
  (101 shorter events, 56.1 us)
Async XLA Ops:
  7.2 145.4 %all-reduce.8.cloned.1.call-start = ((), (), s32[]{:S(2)}) async-start(), calls=%async_computation | async-start | bytes 3538944 | tf_op jit(solution)/shard_map/psum | solution.py:11
  19.0 269.3 %all-reduce.14.cloned.1.call-start = ((), (), s32[]{:S(2)}) async-start(), calls=%async_computation.3 | async-start | bytes 442368 | tf_op jit(solution)/shard_map/psum | solution.py:11
  20.8 426.6 %all-reduce.10.cloned.1.call-start = ((), (), s32[]{:S(2)}) async-start(), calls=%async_computation.1 | async-start | bytes 3538944 | tf_op jit(solution)/shard_map/psum | solution.py:11
  152.6 1.7 copy-start.1
  261.1 339.8 %all-reduce.16.cloned.1.call-start = ((), (), s32[]{:S(2)}) async-start(), calls=%async_computation.4 | async-start | bytes 4423680 | tf_op jit(solution)/shard_map/psum | solution.py:11
  447.4 4.1 copy-start.3
  464.0 2.4 copy-start
  467.8 417.0 %all-reduce.12.cloned.1.call-start = ((), (), s32[]{:S(2)}) async-start(), calls=%async_computation.2 | async-start | bytes 3538944 | tf_op jit(solution)/shard_map/psum | solution.py:11
  600.8 4.4 copy-start.2
  606.5 0.8 copy-start.6
  715.7 3.3 copy-start.5
  897.4 7.0 copy-start.4
  897.4 7.0 copy-start.7
Sparse Core Ops, SparseCore 0:
  19.1 133.4 all-reduce.7
  155.8 132.4 all-reduce.13
  290.9 156.4 all-reduce.9
  467.9 132.8 all-reduce.15
  727.7 156.9 all-reduce.11
where the time goes:
time: 925 us; the launch traced here: 915 us
  waiting for transfers between devices  607 us (66%)
  other arithmetic  190 us (21%)
  matrix products  60.4 us (7%)
  local copies, waits for them, and re-layouts  36.2 us (4%)
  between operations  19.7 us (2%)
    psum x5, waiting for transfers between devices, broadcast(): return lax.psum(kept, axis)  607 us
    another operation x21, other arithmetic, solved_rows(): factor = jnp.linalg.cholesky(pivot_block)  115 us
    another operation x5, other arithmetic, solved_rows(): solved = jax.scipy.linalg.cho_solve((factor, True), rows_local)  61 us
    another operation x20, matrix products, solved_rows(): solved = jax.scipy.linalg.cho_solve((factor, True), rows_local)  22.8 us
  transfers between devices with their start and end apart: 5, of which 5 were waited for; matrix products, arithmetic and copies ran while one was open for 12% of the time, Pallas kernels for 0%

commit v1 on v0

--- a/solution.py
+++ b/solution.py
@@ -2,13 +2,15 @@
 import jax.numpy as jnp
 from jax import lax
 from jax.sharding import PartitionSpec as P
+from jax.lax import all_gather
 
 HEAD = 192
+cells_obtain = lambda x0, named_axis: jnp.sum(all_gather(x0, named_axis), 0)
 
 
 def broadcast(value, axis, source):
     kept = jnp.where(lax.axis_index(axis) == source, value, 0).astype(value.dtype)
-    return lax.psum(kept, axis)
+    return cells_obtain(kept, axis)
 
 
 def per_device(hessian, weight, pairs):

time: 925 us -> 1310 us (1.42)
  waiting for transfers between devices: 607 us -> 970 us
  other arithmetic: 190 us -> 234 us
  local copies, waits for them, and re-layouts: 36.2 us -> 18 us
    all_gather x0 -> x6, waiting for transfers between devices: none -> 970 us  [cells_obtain = lambda x0, named_axis: jnp.sum(all_gather(x0, named_axis), 0)]
    psum x5 -> x0, waiting for transfers between devices: 607 us -> none  [broadcast(): return lax.psum(kept, axis)]
    reduce_sum x0 -> x6, other arithmetic: none -> 50.2 us  [cells_obtain = lambda x0, named_axis: jnp.sum(all_gather(x0, named_axis), 0)]
    unnamed x18 -> x12, local copies, waits for them, and re-layouts: 17.1 us -> 3.93 us
  transfers between devices with their start and end apart: 5 -> 6, of which waited for: 5 -> 5; matrix products, arithmetic and copies ran while one was open for 12% -> 12% of each run, Pallas kernels for 0% -> 0%
where the time goes in v1:
time: 1310 us; the launch traced here: 1290 us
  waiting for transfers between devices  970 us (74%)
  other arithmetic  234 us (18%)
  matrix products  50.7 us (4%)
  between operations  20.3 us (2%)
  local copies, waits for them, and re-layouts  18 us (1%)
    all_gather x6, waiting for transfers between devices, cells_obtain = lambda x0, named_axis: jnp.sum(all_gather(x0, named_axis), 0)  970 us
    another operation x21, other arithmetic, solved_rows(): factor = jnp.linalg.cholesky(pivot_block)  113 us
    another operation x5, other arithmetic, solved_rows(): solved = jax.scipy.linalg.cho_solve((factor, True), rows_local)  59.6 us
    reduce_sum x6, other arithmetic, cells_obtain = lambda x0, named_axis: jnp.sum(all_gather(x0, named_axis), 0)  50.2 us
  transfers between devices with their start and end apart: 6, of which 5 were waited for; matrix products, arithmetic and copies ran while one was open for 12% of the time, Pallas kernels for 0%

profile of v1, /device:TPU:7, one launch (start us, length us, event | category | flops | bytes accessed | tf_op | source)
XLA Modules:
  0.0 1293.3 jit_solution(12046963656399442881)
XLA Ops:
  9.3 3.2 dynamic-slice_select_fusion.1
  12.6 303.9 %all-gather.13.cloned.1.call-done = f32[18432,384]{1,0:T(8,128)} async-done(((f32[1152,384]{1,0:T(8,128)}), f32[18432,384]{1,0:T(8,128)}) %all-gather.13.cloned.1.call-update) | async-done | bytes 28311568 | tf_op jit(solution)/shard_map/all_gather | solution.py:8
  316.5 10.7 reduce_sum.57
  327.9 11.7 cholesky.208
  339.6 9.8 custom-call.22
  350.1 11.7 cholesky.227
  361.8 10.0 custom-call.23
  372.3 11.7 cholesky.246
  387.4 6.0 while.4
  393.4 29.7 %custom-call.24 = f32[3,128,128]{1,2,0:T(8,128)S(1)} custom-call(f32[3,128,128]{2,1,0:T(8,128)S(1)} %get-tuple-element.18), custom_call_target="InvertDiagBlocksLowerTriangular" | custom-call | tf_op jit(solution)/shard_map/jit(_cho_solve)/triangular_solve | solution.py:41
  427.3 1.9 convolution_subtract_fusion.10
  437.2 162.0 %all-gather.15.cloned.1.call-done = f32[6144,1152]{1,0:T(8,128)} async-done(((f32[384,1152]{1,0:T(8,128)}), f32[6144,1152]{1,0:T(8,128)}) %all-gather.15.cloned.1.call-update) | async-done | bytes 28311568 | tf_op jit(solution)/shard_map/all_gather | solution.py:8
  599.3 11.2 reduce_sum.58
  610.5 11.4 convolution_subtract_fusion.1
  621.9 2.4 copy-done
  626.0 40.0 %all-gather.21.cloned.1.call-done = bf16[4608,384]{1,0:T(8,128)(2,1)} async-done(((bf16[288,384]{1,0:T(8,128)(2,1)}), bf16[4608,384]{1,0:T(8,128)(2,1)}) %all-gather.21.cloned.1.call-update) | async-done | bytes 3538960 | tf_op jit(solution)/shard_map/all_gather | solution.py:8
  666.1 2.6 reduce_sum.61
  672.2 303.6 %all-gather.17.cloned.1.call-done = f32[18432,384]{1,0:T(8,128)} async-done(((f32[1152,384]{1,0:T(8,128)}), f32[18432,384]{1,0:T(8,128)}) %all-gather.17.cloned.1.call-update) | async-done | bytes 28311568 | tf_op jit(solution)/shard_map/all_gather | solution.py:8
  975.8 10.8 reduce_sum.59
  987.3 11.7 cholesky.261
  999.1 9.8 custom-call.25
  1009.5 11.7 cholesky.280
  1021.2 10.0 custom-call.26
  1031.7 11.7 cholesky.299
  1047.5 6.0 while.5
  1053.6 29.7 %custom-call.27 = f32[3,128,128]{1,2,0:T(8,128)S(1)} custom-call(f32[3,128,128]{2,1,0:T(8,128)S(1)} %get-tuple-element.19), custom_call_target="InvertDiagBlocksLowerTriangular" | custom-call | tf_op jit(solution)/shard_map/jit(_cho_solve)/triangular_solve | solution.py:41
  1087.5 1.9 convolution_subtract_fusion.6
  1094.8 4.1 reduce_sum.62
  1099.0 160.5 %all-gather.19.cloned.1.call-done = f32[6144,1152]{1,0:T(8,128)} async-done(((f32[384,1152]{1,0:T(8,128)}), f32[6144,1152]{1,0:T(8,128)}) %all-gather.19.cloned.1.call-update) | async-done | bytes 28311568 | tf_op jit(solution)/shard_map/all_gather | solution.py:8
  1259.4 10.7 reduce_sum.60
  1270.2 12.6 convolution_subtract_fusion
  1282.8 3.3 fusion
  (106 shorter events, 46.7 us)
Async XLA Ops:
  7.2 309.3 %all-gather.13.cloned.1.call-start = ((), (), s32[]{:S(2)}) async-start(), calls=%async_computation | async-start | bytes 30081024 | tf_op jit(solution)/shard_map/all_gather | solution.py:8
  12.5 586.7 %all-gather.15.cloned.1.call-start = ((), (), s32[]{:S(2)}) async-start(), calls=%async_computation.1 | async-start | bytes 30081024 | tf_op jit(solution)/shard_map/all_gather | solution.py:8
  434.6 231.4 %all-gather.21.cloned.1.call-start = ((), (), s32[]{:S(2)}) async-start(), calls=%async_computation.4 | async-start | bytes 3760128 | tf_op jit(solution)/shard_map/all_gather | solution.py:8
  436.4 539.3 %all-gather.17.cloned.1.call-start = ((), (), s32[]{:S(2)}) async-start(), calls=%async_computation.2 | async-start | bytes 30081024 | tf_op jit(solution)/shard_map/all_gather | solution.py:8
  621.8 2.4 copy-start
  626.0 468.8 %all-gather.23.cloned.1.call-start = ((), (), s32[]{:S(2)}) async-start(), calls=%async_computation.5 | async-start | bytes 7520256 | tf_op jit(solution)/shard_map/all_gather | solution.py:8
  666.1 2.7 copy-start.4
  670.1 1.1 copy-start.1
  672.1 587.3 %all-gather.19.cloned.1.call-start = ((), (), s32[]{:S(2)}) async-start(), calls=%async_computation.3 | async-start | bytes 30081024 | tf_op jit(solution)/shard_map/all_gather | solution.py:8
  1270.2 12.6 copy-start.2
  1270.2 12.6 copy-start.3
Sparse Core Ops, SparseCore 0:
  12.7 303.8 all-gather.12
  434.7 164.4 all-gather.14
  601.6 64.3 all-gather.20
  667.7 308.0 all-gather.16
  978.0 85.4 all-gather.22
  1094.9 164.4 all-gather.18
